TPU v7x, 256 devices: a whole 4x4x8 slice. The times are simulated.
256 devices in a mesh: fsdp: 32 (over y_hi, z, core), grp: 8 (over y_lo, x).
Axes of the slice: x: 4, y: 4 (y_hi: 2, y_lo: 2; y = y_hi * 2 + y_lo), z: 8, core: 2. Of those that a mesh axis runs over, the one named last changes fastest.
Arguments:
- hidden_act: bfloat16 [8, 2048, 14336], P('grp', None, 'fsdp'), may hold values from -6 to 6
- grad_output: bfloat16 [8, 2048, 4096], P('grp', 'fsdp'), may hold values from -6 to 6
- down_weight: bfloat16 [14336, 4096], P('fsdp'), may hold values from -0.09375 to 0.09375
- proj_in: bfloat16 [14336, 64], P('fsdp'), may hold values from -0.046875 to 0.046875
- proj_out: bfloat16 [4096, 64], replicated, may hold values from -0.09375 to 0.09375
- example_ids: int32 [8, 2048], P('grp'), may hold values from 0 to 7, never falling along the last dimension, each value on 1 to 512 neighbouring positions
Outputs:
- grad_hidden: bfloat16 [8, 2048, 14336], P('grp', None, 'fsdp')
- gram: float32 [4096, 4096], P('grp', 'fsdp')
- scores: float32 [64], replicated
Inputs may be any that keep to these rules, and one draw needn't show every extreme that they name: `example_ids`: never falls along a group's tokens; each of the 8 examples of a group has 1 to 512 tokens, one exactly 512.
All inputs are finite; a program needn't handle non-finite values.
Results may differ from a plain program's by a relative error of at most 0.001.
Values may be sent and summed in bfloat16 or wider, within the bound.
No kernel may reach another device: no remote copies, remote signals or barrier semaphores. Data moves between devices by JAX's collectives and lax.ppermute only.
A program may use at most 128 MiB of HBM per device.

v0:
```python
import jax
import jax.numpy as jnp
from jax import lax
from jax.sharding import PartitionSpec as P

PROJ = 64
TOK_GRP = 2048
EX_GRP = 8


def inverse_diagonal(matrix):
    lower = jnp.linalg.cholesky(matrix)
    eye = jnp.eye(matrix.shape[0], dtype=matrix.dtype)
    lower_inv = jax.scipy.linalg.solve_triangular(lower, eye, lower=True)
    return jnp.sum(lower_inv * lower_inv, axis=0)


def example_features(ids, left, right):
    onehot = (jnp.arange(EX_GRP, dtype=jnp.int32)[:, None] == ids[None, :]).astype(jnp.float32)
    weighted = (onehot[:, None, :] * jnp.transpose(left)[None, :, :]).reshape(
        EX_GRP * PROJ, ids.shape[0]
    )
    product = jnp.dot(weighted, right, precision=lax.Precision.HIGHEST)
    return product.reshape(EX_GRP, PROJ * PROJ) * (EX_GRP / TOK_GRP) ** 0.5


def body(hidden_act, grad_output, down_weight, proj_in, proj_out, example_ids):
    fsdp_count = lax.axis_size("fsdp")
    group_count = lax.axis_size("grp")
    hidden_rows = hidden_act[0]
    grad_rows = grad_output[0]
    group_ids = example_ids[0]
    tok_rows = grad_rows.shape[0]
    feat_width = PROJ * PROJ
    examples = EX_GRP * group_count
    grad_full = lax.all_gather(grad_rows, "fsdp", axis=0, tiled=True)
    grad_hidden = lax.dot_general(
        grad_full, down_weight, (((1,), (1,)), ((), ())), preferred_element_type=jnp.float32
    )
    grad_hidden = grad_hidden.astype(jnp.bfloat16)[None]
    rows_part = hidden_rows
    left = lax.psum_scatter(
        jnp.dot(rows_part, proj_in, preferred_element_type=jnp.float32),
        "fsdp",
        scatter_dimension=0,
        tiled=True,
    )
    right = jnp.dot(grad_rows, proj_out, preferred_element_type=jnp.float32)
    my_ids = lax.dynamic_slice_in_dim(group_ids, lax.axis_index("fsdp") * tok_rows, tok_rows, 0)
    partial_feats = example_features(my_ids, left, right)
    col_count = feat_width // fsdp_count
    group_feats = lax.psum(partial_feats, "fsdp")
    all_feats = lax.all_gather(group_feats.astype(jnp.bfloat16), "grp", axis=0, tiled=True).astype(
        group_feats.dtype
    )
    own_cols = lax.dynamic_slice_in_dim(
        group_feats, lax.axis_index("fsdp") * col_count, col_count, 1
    )
    rows_part = group_feats
    product = lax.dot_general(
        rows_part,
        own_cols,
        (((0,), (0,)), ((), ())),
        precision=lax.Precision.HIGHEST,
        preferred_element_type=jnp.float32,
    )
    gram = lax.psum_scatter(product / examples, "grp", scatter_dimension=0, tiled=True)
    kernel = lax.dot_general(
        all_feats,
        all_feats,
        (((1,), (1,)), ((), ())),
        precision=lax.Precision.HIGHEST,
        preferred_element_type=jnp.float32,
    )
    ridge = jnp.trace(kernel) / examples
    eye = jnp.eye(examples, dtype=jnp.float32)
    scores = 1.0 - ridge * inverse_diagonal(kernel + ridge * eye)
    return (grad_hidden, gram, scores)


def solution(mesh):
    in_specs = (
        P("grp", None, "fsdp"),
        P("grp", "fsdp", None),
        P("fsdp", None),
        P("fsdp", None),
        P(),
        P("grp", None),
    )
    out_specs = (P("grp", None, "fsdp"), P("grp", "fsdp"), P())
    return jax.shard_map(body, mesh=mesh, in_specs=in_specs, out_specs=out_specs, check_vma=False)
```

profile of v0, /device:TPU:32, one launch (start us, length us, event | category | flops | bytes accessed | tf_op | source)
XLA Modules:
  0.0 566.4 jit_solution(12416813345016848578)
XLA Ops:
  7.2 1.4 copy-done
  8.7 2.6 fusion.8
  11.3 0.7 dynamic-slice_bitcast_fusion
  12.1 0.3 fusion.11
  12.4 117.4 %reduce-scatter.3.cloned.1.call-done = f32[64,64]{1,0:T(8,128)} async-done(((f32[2048,64]{1,0:T(8,128)}), f32[64,64]{1,0:T(8,128)}) %reduce-scatter.3.cloned.1.call-update) | async-done | bytes 16400 | tf_op jit(solution)/shard_map/reduce_scatter | solution.py:42
  129.8 0.8 copy.11
  130.7 0.4 convolution_multiply_fusion.1
  131.1 0.1 copy.12
  131.2 0.8 mul.56
  132.1 0.7 all-gather.3.cloned.1.call-update
  132.8 239.1 %all-reduce.2.cloned.1.call-done = f32[8,4096]{1,0:T(8,128)} async-done(((f32[8,4096]{1,0:T(8,128)}), f32[8,4096]{1,0:T(8,128)}) %all-reduce.2.cloned.1.call-update) | async-done | bytes 131088 | tf_op jit(solution)/shard_map/psum | solution.py:52
  371.9 5.8 %convolution_multiply_fusion = f32[4096,128]{1,0:T(8,128)} fusion(f32[8,4096]{1,0:T(8,128)} %all-reduce.2.cloned.1.call-done, s32[]{:T(128)S(6)} %select_n.16), kind=kOutput, calls=%fused_computation.2 | convolution fusion | flops 50855936 | bytes 2232324 | tf_op jit(solution)/shard_map/dot_general | solution.py:60
  377.7 29.4 %all_gather.7 = bf16[64,4096]{1,0:T(8,128)(2,1)S(1)} all-gather(bf16[8,4096]{1,0:T(8,128)(2,1)S(1)} %convert_element_type.18), channel_id=1, replica_groups=mesh['fsdp'=32,'grp'=8] {'grp'}, dimensions={0}, use_global_device_ids=true | all-gather | bytes 589824 | tf_op jit(solution)/shard_map/all_gather | solution.py:53
  407.1 0.9 select_reduce_fusion.1
  408.0 0.1 copy.13
  408.7 5.8 %cholesky.13 = f32[64,64]{1,0:T(8,128)S(1)} custom-call(f32[64,64]{1,0:T(8,128)S(1)} %fusion.16), custom_call_target="Cholesky" | custom-call | tf_op jit(solution)/shard_map/jit(cholesky)/cholesky | solution.py:12
  414.6 0.6 compare_reduce_fusion
  415.3 0.7 fusion.13
  415.9 4.9 custom-call.7
  420.8 0.2 fusion.10
  421.1 0.5 multiply_subtract_fusion
  421.6 91.2 %all-gather.3.cloned.1.call-done = bf16[1,2048,4096]{2,1,0:T(8,128)(2,1)} async-done(((bf16[1,64,4096]{2,1,0:T(8,128)(2,1)}), bf16[1,2048,4096]{2,1,0:T(8,128)(2,1)}) %all-gather.3.cloned.1.call-update) | async-done | bytes 16777232 | tf_op jit(solution)/shard_map/all_gather | solution.py:36
  512.8 13.3 %fusion.5 = bf16[1,2048,448]{1,2,0:T(8,128)(2,1)} fusion(bf16[448,4096]{1,0:T(8,128)(2,1)} %param.8, bf16[1,2048,4096]{2,1,0:T(8,128)(2,1)} %all-gather.3.cloned.1.call-done), kind=kOutput, calls=%fused_computation.4 | convolution fusion | flops 7517110272 | bytes 22282240 | tf_op jit(solution)/shard_map/dot_general | solution.py:37
  526.2 33.7 %reduce-scatter.5.cloned.1.call-done = f32[512,128]{1,0:T(8,128)} async-done(((f32[4096,128]{1,0:T(8,128)}), f32[512,128]{1,0:T(8,128)}) %reduce-scatter.5.cloned.1.call-update) | async-done | bytes 262160 | tf_op jit(solution)/shard_map/reduce_scatter | solution.py:67
  (19 shorter events, 0.3 us)
Async XLA Ops:
  7.2 1.5 copy-start
  7.2 4.9 copy-start.1
  7.2 4.9 copy-start.3
  7.2 122.6 %reduce-scatter.3.cloned.1.call-start = ((), (), s32[]{:S(2)}) async-start(), calls=%async_computation.2 | async-start | bytes 1081344 | tf_op jit(solution)/shard_map/reduce_scatter | solution.py:42
  11.3 360.6 %all-reduce.2.cloned.1.call-start = ((), (), s32[]{:S(2)}) async-start(), calls=%async_computation.3 | async-start | bytes 262144 | tf_op jit(solution)/shard_map/psum | solution.py:52
  132.0 380.8 %all-gather.3.cloned.1.call-start = ((), (), s32[]{:S(2)}) async-start(), calls=%async_computation.5 | async-start | bytes 17301504 | tf_op jit(solution)/shard_map/all_gather | solution.py:36
  132.8 427.1 %reduce-scatter.5.cloned.1.call-start = ((), (), s32[]{:S(2)}) async-start(), calls=%async_computation.4 | async-start | bytes 2359296 | tf_op jit(solution)/shard_map/reduce_scatter | solution.py:67
  371.9 5.8 %copy-start.2 = (f32[8,4096]{1,0:T(8,128)S(1)}, f32[8,4096]{1,0:T(8,128)}, u32[]{:S(2)}) copy-start(f32[8,4096]{1,0:T(8,128)} %all-reduce.2.cloned.1.call-done) | copy-start | bytes 393220
Sparse Core Ops, SparseCore 0:
  12.7 117.0 reduce-scatter.2
  133.2 238.6 all-reduce.1
  374.7 138.1 all-gather.2
  515.8 43.9 reduce-scatter.4
where the time goes:
time: 567 us; the launch traced here: 566 us
  waiting for transfers between devices  482 us (85%)
  blocking collectives  29.4 us (5%)
  matrix products  23.5 us (4%)
  between operations  14.5 us (3%)
  other arithmetic  12.6 us (2%)
    psum x1, waiting for transfers between devices, body(): group_feats = lax.psum(partial_feats, 'fsdp')  239 us
    reduce_scatter x1, waiting for transfers between devices, body(): lax.psum_scatter(jnp.dot(rows_part, proj_in, preferred_element_type=jnp.f...  117 us
    all_gather x1, waiting for transfers between devices, body(): grad_full = lax.all_gather(grad_rows, 'fsdp', axis=0, tiled=True)  91.2 us
    reduce_scatter x1, waiting for transfers between devices, body(): lax.psum_scatter(product / examples, 'grp', scatter_dimension=0, tiled=True)  33.7 us
    all_gather x1, blocking collectives, body(): lax.all_gather(group_feats.astype(jnp.bfloat16), 'grp', axis=0, tiled=True)  29.4 us
    dot_general x1, matrix products, body(): lax.dot_general(grad_full, down_weight, (((1,), (1,)), ((), ())), preferr...  13.3 us
  transfers between devices with their start and end apart: 4, of which 4 were waited for; matrix products, arithmetic and copies ran while one was open for 6% of the time, Pallas kernels for 0%

commit v1 on v0

--- a/solution.py
+++ b/solution.py
@@ -49,7 +49,7 @@
     my_ids = lax.dynamic_slice_in_dim(group_ids, lax.axis_index("fsdp") * tok_rows, tok_rows, 0)
     partial_feats = example_features(my_ids, left, right)
     col_count = feat_width // fsdp_count
-    group_feats = lax.psum(partial_feats, "fsdp")
+    group_feats = jnp.sum(lax.all_gather(partial_feats, "fsdp"), axis=0)
     all_feats = lax.all_gather(group_feats.astype(jnp.bfloat16), "grp", axis=0, tiled=True).astype(
         group_feats.dtype
     )

time: 567 us -> 410 us (0.72)
  waiting for transfers between devices: 482 us -> 325 us
    psum x1 -> x0, waiting for transfers between devices: 239 us -> none  [body(): group_feats = lax.psum(partial_feats, 'fsdp')]
    all_gather x0 -> x1, waiting for transfers between devices: none -> 85.8 us  [body(): group_feats = jnp.sum(lax.all_gather(partial_feats, 'fsdp'), axis=0)]
  transfers between devices with their start and end apart: 4 -> 4, of which waited for: 4 -> 4; matrix products, arithmetic and copies ran while one was open for 6% -> 9% of each run, Pallas kernels for 0% -> 0%
where the time goes in v1:
time: 410 us
  waiting for transfers between devices  325 us (79%)
  blocking collectives  29.1 us (7%)
  matrix products  22.5 us (5%)
  other arithmetic  15 us (4%)
  between operations  14.5 us (4%)
    reduce_scatter x1, waiting for transfers between devices, body(): lax.psum_scatter(jnp.dot(rows_part, proj_in, preferred_element_type=jnp.f...  117 us
    all_gather x1, waiting for transfers between devices, body(): grad_full = lax.all_gather(grad_rows, 'fsdp', axis=0, tiled=True)  87 us
    all_gather x1, waiting for transfers between devices, body(): group_feats = jnp.sum(lax.all_gather(partial_feats, 'fsdp'), axis=0)  85.8 us
    reduce_scatter x1, waiting for transfers between devices, body(): lax.psum_scatter(product / examples, 'grp', scatter_dimension=0, tiled=True)  33.7 us
    all_gather x1, blocking collectives, body(): lax.all_gather(group_feats.astype(jnp.bfloat16), 'grp', axis=0, tiled=True)  29.1 us
    dot_general x1, matrix products, body(): lax.dot_general(grad_full, down_weight, (((1,), (1,)), ((), ())), preferr...  13.3 us
  transfers between devices with their start and end apart: 4, of which 4 were waited for; matrix products, arithmetic and copies ran while one was open for 9% of the time, Pallas kernels for 0%

profile of v1, /device:TPU:32, one launch (start us, length us, event | category | flops | bytes accessed | tf_op | source)
XLA Modules:
  0.0 410.0 jit_solution(5372258330692015725)
XLA Ops:
  7.2 1.4 copy-done
  8.7 2.6 fusion.8
  11.3 0.7 dynamic-slice_bitcast_fusion
  12.1 0.3 fusion.11
  12.4 117.4 %reduce-scatter.3.cloned.1.call-done = f32[64,64]{1,0:T(8,128)} async-done(((f32[2048,64]{1,0:T(8,128)}), f32[64,64]{1,0:T(8,128)}) %reduce-scatter.3.cloned.1.call-update) | async-done | bytes 16400 | tf_op jit(solution)/shard_map/reduce_scatter | solution.py:42
  129.8 0.8 copy.14
  130.7 0.4 convolution_multiply_fusion.1
  131.1 0.1 copy.15
  131.2 0.8 mul.63
  132.1 0.7 all-gather.6.cloned.1.call-update
  132.8 85.8 %all-gather.4.cloned.1.call-done = f32[32,8,4096]{2,1,0:T(8,128)} async-done(((f32[1,8,4096]{2,1,0:T(8,128)}), f32[32,8,4096]{2,1,0:T(8,128)}) %all-gather.4.cloned.1.call-update) | async-done | bytes 4194320 | tf_op jit(solution)/shard_map/all_gather | solution.py:52
  218.6 2.4 reduce_sum.28
  221.0 4.8 %convolution_multiply_fusion = f32[4096,128]{1,0:T(8,128)} fusion(f32[8,4096]{1,0:T(8,128)S(1)} %reduce_sum.28, s32[]{:T(128)S(6)} %select_n.16), kind=kOutput, calls=%fused_computation.2 | convolution fusion | flops 50855936 | bytes 2232324 | tf_op jit(solution)/shard_map/dot_general | solution.py:60
  225.9 29.1 %all_gather.12 = bf16[64,4096]{1,0:T(8,128)(2,1)S(1)} all-gather(bf16[8,4096]{1,0:T(8,128)(2,1)S(1)} %convert_element_type.18), channel_id=1, replica_groups=mesh['fsdp'=32,'grp'=8] {'grp'}, dimensions={0}, use_global_device_ids=true | all-gather | bytes 589824 | tf_op jit(solution)/shard_map/all_gather | solution.py:53
  254.9 0.9 select_reduce_fusion.1
  256.6 5.8 %cholesky.13 = f32[64,64]{1,0:T(8,128)S(1)} custom-call(f32[64,64]{1,0:T(8,128)S(1)} %fusion.16), custom_call_target="Cholesky" | custom-call | tf_op jit(solution)/shard_map/jit(cholesky)/cholesky | solution.py:12
  262.5 0.6 compare_reduce_fusion
  263.1 0.7 fusion.13
  263.8 4.9 %custom-call.7 = f32[1,64,64]{1,2,0:T(8,128)S(1)} custom-call(f32[1,64,64]{2,1,0:T(8,128)S(1)} %fusion.13), custom_call_target="InvertDiagBlocksLowerTriangular" | custom-call | tf_op jit(solution)/shard_map/jit(_solve_triangular)/triangular_solve | solution.py:14
  268.7 0.2 fusion.10
  268.9 0.5 multiply_subtract_fusion
  269.4 87.0 %all-gather.6.cloned.1.call-done = bf16[1,2048,4096]{2,1,0:T(8,128)(2,1)} async-done(((bf16[1,64,4096]{2,1,0:T(8,128)(2,1)}), bf16[1,2048,4096]{2,1,0:T(8,128)(2,1)}) %all-gather.6.cloned.1.call-update) | async-done | bytes 16777232 | tf_op jit(solution)/shard_map/all_gather | solution.py:36
  356.5 13.3 %fusion.5 = bf16[1,2048,448]{1,2,0:T(8,128)(2,1)} fusion(bf16[448,4096]{1,0:T(8,128)(2,1)} %param.8, bf16[1,2048,4096]{2,1,0:T(8,128)(2,1)} %all-gather.6.cloned.1.call-done), kind=kOutput, calls=%fused_computation.4 | convolution fusion | flops 7517110272 | bytes 22282240 | tf_op jit(solution)/shard_map/dot_general | solution.py:37
  369.8 33.7 %reduce-scatter.5.cloned.1.call-done = f32[512,128]{1,0:T(8,128)} async-done(((f32[4096,128]{1,0:T(8,128)}), f32[512,128]{1,0:T(8,128)}) %reduce-scatter.5.cloned.1.call-update) | async-done | bytes 262160 | tf_op jit(solution)/shard_map/reduce_scatter | solution.py:67
  (18 shorter events, 0.4 us)
Async XLA Ops:
  7.2 1.5 copy-start
  7.2 4.9 %copy-start.1 = (bf16[1,64,4096]{2,1,0:T(8,128)(2,1)S(1)}, bf16[1,64,4096]{2,1,0:T(8,128)(2,1)}, u32[]{:S(2)}) copy-start(bf16[1,64,4096]{2,1,0:T(8,128)(2,1)} %param.7) | copy-start | bytes 1572868
  7.2 4.9 %copy-start.2 = (bf16[4096,64]{0,1:T(8,128)(2,1)S(1)}, bf16[4096,64]{0,1:T(8,128)(2,1)}, u32[]{:S(2)}) copy-start(bf16[4096,64]{0,1:T(8,128)(2,1)} %param.10) | copy-start | bytes 1572868
  7.2 122.6 %reduce-scatter.3.cloned.1.call-start = ((), (), s32[]{:S(2)}) async-start(), calls=%async_computation.2 | async-start | bytes 1081344 | tf_op jit(solution)/shard_map/reduce_scatter | solution.py:42
  11.3 207.3 %all-gather.4.cloned.1.call-start = ((), (), s32[]{:S(2)}) async-start(), calls=%async_computation.3 | async-start | bytes 4325376 | tf_op jit(solution)/shard_map/all_gather | solution.py:52
  132.0 224.4 %all-gather.6.cloned.1.call-start = ((), (), s32[]{:S(2)}) async-start(), calls=%async_computation.5 | async-start | bytes 17301504 | tf_op jit(solution)/shard_map/all_gather | solution.py:36
  132.8 270.7 %reduce-scatter.5.cloned.1.call-start = ((), (), s32[]{:S(2)}) async-start(), calls=%async_computation.4 | async-start | bytes 2359296 | tf_op jit(solution)/shard_map/reduce_scatter | solution.py:67
Sparse Core Ops, SparseCore 0:
  12.7 117.0 reduce-scatter.2
  133.5 85.0 all-gather.3
  221.8 134.6 all-gather.5
  359.6 43.8 reduce-scatter.4
